TPU v7x, 32 devices: a whole 2x2x4 slice. The times are simulated.
32 devices in a mesh: rep: 8 (over y, x, core), shard: 4 (over z).
Axes of the slice: x: 2, y: 2, z: 4, core: 2. Of those that a mesh axis runs over, the one named last changes fastest.
Arguments:
- block_in: float32 [4096, 1024], P(('rep', 'shard')), may hold values from -6 to 6
- cotangent: float32 [4096, 1024], P(('rep', 'shard')), may hold values from -0.09375 to 0.09375
- segments: int32 [8, 512], P('rep'), may hold values from 0 to 3, never falling along the last dimension, each value on 1 to 224 neighbouring positions
- qkv_weight: float32 [1024, 3072], P(('rep', 'shard')), may hold values from -0.1875 to 0.1875
- out_weight: float32 [1024, 1024], P(('rep', 'shard')), may hold values from -0.75 to 0.75
- up_weight: float32 [1024, 4096], P(('rep', 'shard')), may hold values from -0.1875 to 0.1875
- down_weight: float32 [4096, 1024], P(('rep', 'shard')), may hold values from -0.09375 to 0.09375
- vectors: float32 [13, 1024], P(None, ('rep', 'shard')), may hold values from -0.9 to 1.5, as said below
- first_qkv: float32 [1024, 3072], P(('rep', 'shard')), may hold values from -1.8 to 1.8
- first_out: float32 [1024, 1024], P(('rep', 'shard')), may hold values from -1.8 to 1.8
- first_up: float32 [1024, 4096], P(('rep', 'shard')), may hold values from -1.8 to 1.8
- first_down: float32 [4096, 1024], P(('rep', 'shard')), may hold values from -1.8 to 1.8
- first_vec: float32 [13, 1024], P(None, ('rep', 'shard')), may hold values from -1.8 to 1.8
- second_qkv: float32 [1024, 3072], P(('rep', 'shard')), may hold values from 0.002 to 0.2
- second_out: float32 [1024, 1024], P(('rep', 'shard')), may hold values from 0.002 to 0.2
- second_up: float32 [1024, 4096], P(('rep', 'shard')), may hold values from 0.002 to 0.2
- second_down: float32 [4096, 1024], P(('rep', 'shard')), may hold values from 0.002 to 0.2
- second_vec: float32 [13, 1024], P(None, ('rep', 'shard')), may hold values from 0.002 to 0.2
Outputs:
- block_out: float32 [4096, 1024], P(('rep', 'shard'))
- grad_input: float32 [4096, 1024], P(('rep', 'shard'))
- grad_qkv: float32 [1024, 3072], P(('rep', 'shard'))
- grad_out: float32 [1024, 1024], P(('rep', 'shard'))
- grad_up: float32 [1024, 4096], P(('rep', 'shard'))
- grad_down: float32 [4096, 1024], P(('rep', 'shard'))
- grad_vec: float32 [13, 1024], P(None, ('rep', 'shard'))
- new_qkv: float32 [1024, 3072], P(('rep', 'shard'))
- new_out: float32 [1024, 1024], P(('rep', 'shard'))
- new_up: float32 [1024, 4096], P(('rep', 'shard'))
- new_down: float32 [4096, 1024], P(('rep', 'shard'))
- new_vec: float32 [13, 1024], P(None, ('rep', 'shard'))
- new_first_qkv: float32 [1024, 3072], P(('rep', 'shard'))
- new_first_out: float32 [1024, 1024], P(('rep', 'shard'))
- new_first_up: float32 [1024, 4096], P(('rep', 'shard'))
- new_first_down: float32 [4096, 1024], P(('rep', 'shard'))
- new_first_vec: float32 [13, 1024], P(None, ('rep', 'shard'))
- new_second_qkv: float32 [1024, 3072], P(('rep', 'shard'))
- new_second_out: float32 [1024, 1024], P(('rep', 'shard'))
- new_second_up: float32 [1024, 4096], P(('rep', 'shard'))
- new_second_down: float32 [4096, 1024], P(('rep', 'shard'))
- new_second_vec: float32 [13, 1024], P(None, ('rep', 'shard'))
Inputs may be any that keep to these rules, and one draw needn't show every extreme that they name: `segments`: in every row the segment numbers never fall; each of the 4 numbers covers 1 to 224 consecutive positions and one covers exactly 224. `vectors`: rows 0 and 2 lie in 0.5 to 1.5.
All inputs are finite; a program needn't handle non-finite values.
Results may differ from a plain program's by a relative error of at most 0.019.
The roundings to bfloat16 on the way count: a program that leaves them out, or rounds other values in their place, can miss the bound.
Values may be sent and summed in bfloat16 or wider, within the bound.
No kernel may reach another device: no remote copies, remote signals or barrier semaphores. Data moves between devices by JAX's collectives and lax.ppermute only.
A program may use at most 320 MiB of HBM per device.

v0:
```python
import jax
import jax.numpy as jnp
from jax import lax
from jax.sharding import PartitionSpec as P

D = 1024
HEADS = 16
FF = 4096
ROT = 16
STEP = 10
LN_EPS = 1e-05
BETA_ONE = 0.9
BETA_TWO = 0.95
ADAM_EPS = 1e-08
LR_MATRIX = 0.03
LR_VECTOR = 0.2
WEIGHT_DECAY = 0.01
ROPE_BASE = 10000.0
INV_ROOT_TWO = 0.7071067811865476
INV_ROOT_TAU = 0.3989422804014327


def layer_norm(values, gain, shift):
    center = values - jnp.mean(values, axis=-1, keepdims=True)
    inv_std = lax.rsqrt(jnp.mean(center * center, axis=-1, keepdims=True) + LN_EPS)
    normed = center * inv_std
    return (normed * gain + shift, normed, inv_std)


def norm_backward(upstream, normed, inv_std, gain):
    scaled = upstream * gain
    result = inv_std * (
        scaled
        - jnp.mean(scaled, axis=-1, keepdims=True)
        - normed * jnp.mean(scaled * normed, axis=-1, keepdims=True)
    )
    return (result, jnp.sum(upstream * normed, axis=0), jnp.sum(upstream, axis=0))


def rope_tables(positions):
    half_rot = ROT // 2
    freqs = ROPE_BASE ** (-(2.0 * jnp.arange(half_rot).astype(jnp.float32) / ROT))
    angles = positions.astype(jnp.float32)[:, None] * freqs[None, :]
    return (jnp.cos(angles)[:, None, :], jnp.sin(angles)[:, None, :])


def rotate(heads, cosines, sines):
    half_rot = ROT // 2
    lower = heads[..., :half_rot]
    upper = heads[..., half_rot:ROT]
    return jnp.concatenate(
        [lower * cosines - upper * sines, upper * cosines + lower * sines, heads[..., ROT:]],
        axis=-1,
    )


def unrotate(heads, cosines, sines):
    half_rot = ROT // 2
    lower = heads[..., :half_rot]
    upper = heads[..., half_rot:ROT]
    return jnp.concatenate(
        [lower * cosines + upper * sines, upper * cosines - lower * sines, heads[..., ROT:]],
        axis=-1,
    )


def gelu_value(inner):
    return 0.5 * inner * (1.0 + jax.scipy.special.erf(inner * INV_ROOT_TWO))


def gelu_slope(inner):
    return (
        0.5 * (1.0 + jax.scipy.special.erf(inner * INV_ROOT_TWO))
        + inner * jnp.exp(-0.5 * inner * inner) * INV_ROOT_TAU
    )


def adam_update(param, grad, first, second, rate, decay):
    first_new = BETA_ONE * first + (1.0 - BETA_ONE) * grad
    second_new = BETA_TWO * second + (1.0 - BETA_TWO) * grad * grad
    first_hat = first_new / (1.0 - BETA_ONE**STEP)
    second_hat = second_new / (1.0 - BETA_TWO**STEP)
    return (
        param - rate * (first_hat / (jnp.sqrt(second_hat) + ADAM_EPS) + decay * param),
        first_new,
        second_new,
    )


def contract_rows(left, right):
    return lax.dot_general(
        left, right, (((0,), (0,)), ((), ())), preferred_element_type=jnp.float32
    )


def contract_cols(left, right):
    return lax.dot_general(
        left, right, (((1,), (1,)), ((), ())), preferred_element_type=jnp.float32
    )


def shards(
    block_in,
    cotangent,
    segments,
    qkv_weight,
    out_weight,
    up_weight,
    down_weight,
    vectors,
    first_qkv,
    first_out,
    first_up,
    first_down,
    first_vec,
    second_qkv,
    second_out,
    second_up,
    second_down,
    second_vec,
):
    bf16 = jnp.bfloat16
    tok_count = block_in.shape[0]
    n_shard = lax.axis_size("shard")
    seq_len = tok_count * n_shard
    head_dim = D // HEADS
    per_row = FF // D
    own_rows = qkv_weight.shape[0]
    score_scale = head_dim ** (-0.5)
    vec_all = lax.all_gather(vectors, ("rep", "shard"), axis=1, tiled=True)
    gain_one, shift_one, gain_two, shift_two = (vec_all[0], vec_all[1], vec_all[2], vec_all[3])
    qkv_bias = vec_all[4:7].reshape(3 * D)
    out_bias = vec_all[7]
    up_bias = vec_all[8 : 8 + per_row].reshape(FF)
    down_bias = vec_all[8 + per_row]
    ln_one, normed_one, inv_one = layer_norm(block_in, gain_one, shift_one)
    ln_two, normed_two, inv_two = layer_norm(block_in, gain_two, shift_two)
    h_one = ln_one.astype(bf16)
    h_two = ln_two.astype(bf16)
    in_table = jnp.concatenate([qkv_weight.astype(bf16), up_weight.astype(bf16)], axis=1)
    out_table = jnp.concatenate(
        [out_weight.astype(bf16), down_weight.astype(bf16).reshape(own_rows, per_row * D)], axis=1
    )
    in_whole = lax.all_gather(in_table, ("rep", "shard"), axis=0, tiled=True)
    qkv_lin = jnp.dot(h_one, in_whole[:, : 3 * D], preferred_element_type=jnp.float32) + qkv_bias
    up_lin = jnp.dot(h_two, in_whole[:, 3 * D :], preferred_element_type=jnp.float32) + up_bias
    offset = lax.axis_index("shard") * tok_count
    query_pos = offset + jnp.arange(tok_count)
    key_pos = jnp.arange(seq_len)
    cosines, sines = rope_tables(query_pos)
    query16 = rotate(qkv_lin[:, :D].reshape(tok_count, HEADS, head_dim), cosines, sines).astype(
        bf16
    )
    key16 = (
        rotate(qkv_lin[:, D : 2 * D].reshape(tok_count, HEADS, head_dim), cosines, sines)
        .reshape(tok_count, D)
        .astype(bf16)
    )
    value16 = qkv_lin[:, 2 * D :].astype(bf16)
    keys_all, values_all = (
        lax.all_gather(key16, "shard", axis=0, tiled=True),
        lax.all_gather(value16, "shard", axis=0, tiled=True),
    )
    keys3 = keys_all.reshape(seq_len, HEADS, head_dim)
    values3 = values_all.reshape(seq_len, HEADS, head_dim)
    seg_row = segments[0]
    seg_query = lax.dynamic_slice_in_dim(seg_row, offset, tok_count)
    allowed = (seg_query[:, None] == seg_row[None, :]) & (key_pos[None, :] <= query_pos[:, None])
    scores = jnp.where(
        allowed[None],
        jnp.einsum("qhd,khd->hqk", query16, keys3, preferred_element_type=jnp.float32)
        * score_scale,
        -jnp.inf,
    )
    row_max = jnp.max(scores, axis=-1, keepdims=True)
    expo = jnp.exp(scores - row_max)
    row_sum = jnp.sum(expo, axis=-1, keepdims=True)
    log_total = row_max + jnp.log(row_sum)
    probs16 = (expo / row_sum).astype(bf16)
    mixed16 = (
        jnp.einsum("hqk,khd->qhd", probs16, values3, preferred_element_type=jnp.float32)
        .reshape(tok_count, D)
        .astype(bf16)
    )
    act16 = gelu_value(up_lin).astype(bf16)
    act3 = act16.reshape(tok_count, D, per_row)
    out_whole = lax.all_gather(out_table, ("rep", "shard"), axis=0, tiled=True)
    branches = jnp.dot(mixed16, out_whole[:, :D], preferred_element_type=jnp.float32)
    branches = branches + jnp.dot(
        act16, out_whole[:, D:].reshape(FF, D), preferred_element_type=jnp.float32
    )
    block_out = block_in + branches + out_bias + down_bias
    upstream16 = cotangent.astype(bf16)
    piece = lax.all_gather(out_table, ("rep", "shard"), axis=0, tiled=True)
    num_rows = piece.shape[0]
    first_part = contract_cols(upstream16, piece[:, :D])
    second_part = contract_cols(upstream16, piece[:, D:].reshape(num_rows * per_row, D)).reshape(
        tok_count, num_rows, per_row
    )
    back_table = jnp.concatenate([first_part[:, :, None], second_part], axis=2)
    d_mixed = back_table[:, :, 0]
    d_act = back_table[:, :, 1:].reshape(tok_count, FF)
    d_up = d_act * gelu_slope(up_lin)
    d_up16 = d_up.astype(bf16)
    d_mixed16 = d_mixed.astype(bf16).reshape(tok_count, HEADS, head_dim)
    row_delta = jnp.sum(
        d_mixed16.astype(jnp.float32)
        * mixed16.reshape(tok_count, HEADS, head_dim).astype(jnp.float32),
        axis=-1,
    ).T[:, :, None]
    scores_again = jnp.where(
        allowed[None],
        jnp.einsum("qhd,khd->hqk", query16, keys3, preferred_element_type=jnp.float32)
        * score_scale,
        -jnp.inf,
    )
    probs_again = jnp.exp(scores_again - log_total)
    d_probs = jnp.einsum("qhd,khd->hqk", d_mixed16, values3, preferred_element_type=jnp.float32)
    d_scores16 = (probs_again * (d_probs - row_delta) * score_scale).astype(bf16)
    probs_back16 = probs_again.astype(bf16)
    d_query = jnp.einsum("hqk,khd->qhd", d_scores16, keys3, preferred_element_type=jnp.float32)
    d_keys = jnp.einsum(
        "hqk,qhd->khd", d_scores16, query16, preferred_element_type=jnp.float32
    ).reshape(seq_len, D)
    d_values = jnp.einsum(
        "hqk,qhd->khd", probs_back16, d_mixed16, preferred_element_type=jnp.float32
    ).reshape(seq_len, D)
    own_dkeys, own_dvalues = (
        lax.psum_scatter(d_keys, "shard", scatter_dimension=0, tiled=True),
        lax.psum_scatter(d_values, "shard", scatter_dimension=0, tiled=True),
    )
    d_qkv = jnp.concatenate(
        [
            unrotate(d_query, cosines, sines).reshape(tok_count, D),
            unrotate(own_dkeys.reshape(tok_count, HEADS, head_dim), cosines, sines).reshape(
                tok_count, D
            ),
            own_dvalues,
        ],
        axis=1,
    )
    d_qkv16 = d_qkv.astype(bf16)
    piece = lax.all_gather(in_table, ("rep", "shard"), axis=0, tiled=True)
    first_part = contract_cols(d_qkv16, piece[:, : 3 * D])
    second_part = contract_cols(d_up16, piece[:, 3 * D :])
    norm_table = jnp.stack([first_part, second_part], axis=2)
    d_one = norm_table[:, :, 0]
    d_two = norm_table[:, :, 1]
    dx_one, dgain_one, dshift_one = norm_backward(d_one, normed_one, inv_one, gain_one)
    dx_two, dgain_two, dshift_two = norm_backward(d_two, normed_two, inv_two, gain_two)
    grad_input = cotangent + dx_one + dx_two
    cot_sum = jnp.sum(cotangent, axis=0)
    vec_terms = jnp.concatenate(
        [
            dgain_one[None],
            dshift_one[None],
            dgain_two[None],
            dshift_two[None],
            jnp.sum(d_qkv, axis=0).reshape(3, D),
            cot_sum[None],
            jnp.sum(d_up, axis=0).reshape(per_row, D),
            cot_sum[None],
        ],
        axis=0,
    )
    grad_vec = lax.psum_scatter(vec_terms, ("rep", "shard"), scatter_dimension=1, tiled=True)
    one_cols = h_one[:, :, None]
    two_cols = h_two[:, :, None]
    mixed_cols = mixed16[:, :, None]
    term_qkv = contract_rows(one_cols.reshape(tok_count, D), d_qkv16)
    term_up = contract_rows(two_cols.reshape(tok_count, D), d_up16)
    term_out = contract_rows(mixed_cols.reshape(tok_count, D), upstream16)
    term_down = contract_rows(act3.reshape(tok_count, D * per_row), upstream16)
    grad_table = lax.psum_scatter(
        jnp.concatenate([term_qkv, term_up, term_out, term_down.reshape(D, per_row * D)], axis=1),
        ("rep", "shard"),
        scatter_dimension=0,
        tiled=True,
    )
    grad_qkv = grad_table[:, : 3 * D]
    grad_up = grad_table[:, 3 * D : 3 * D + FF]
    grad_out = grad_table[:, 3 * D + FF : 4 * D + FF]
    grad_down = grad_table[:, 4 * D + FF :].reshape(own_rows * per_row, D)
    new_qkv, new_first_qkv, new_second_qkv = adam_update(
        qkv_weight, grad_qkv, first_qkv, second_qkv, LR_MATRIX, WEIGHT_DECAY
    )
    new_out, new_first_out, new_second_out = adam_update(
        out_weight, grad_out, first_out, second_out, LR_MATRIX, WEIGHT_DECAY
    )
    new_up, new_first_up, new_second_up = adam_update(
        up_weight, grad_up, first_up, second_up, LR_MATRIX, WEIGHT_DECAY
    )
    new_down, new_first_down, new_second_down = adam_update(
        down_weight, grad_down, first_down, second_down, LR_MATRIX, WEIGHT_DECAY
    )
    new_vec, new_first_vec, new_second_vec = adam_update(
        vectors, grad_vec, first_vec, second_vec, LR_VECTOR, 0.0
    )
    return (
        block_out,
        grad_input,
        grad_qkv,
        grad_out,
        grad_up,
        grad_down,
        grad_vec,
        new_qkv,
        new_out,
        new_up,
        new_down,
        new_vec,
        new_first_qkv,
        new_first_out,
        new_first_up,
        new_first_down,
        new_first_vec,
        new_second_qkv,
        new_second_out,
        new_second_up,
        new_second_down,
        new_second_vec,
    )


def solution(mesh):
    return jax.shard_map(
        shards,
        mesh=mesh,
        in_specs=(
            P(("rep", "shard"), None),
            P(("rep", "shard"), None),
            P("rep", None),
            P(("rep", "shard"), None),
            P(("rep", "shard"), None),
            P(("rep", "shard"), None),
            P(("rep", "shard"), None),
            P(None, ("rep", "shard")),
            P(("rep", "shard"), None),
            P(("rep", "shard"), None),
            P(("rep", "shard"), None),
            P(("rep", "shard"), None),
            P(None, ("rep", "shard")),
            P(("rep", "shard"), None),
            P(("rep", "shard"), None),
            P(("rep", "shard"), None),
            P(("rep", "shard"), None),
            P(None, ("rep", "shard")),
        ),
        out_specs=(
            P(("rep", "shard"), None),
            P(("rep", "shard"), None),
            P(("rep", "shard"), None),
            P(("rep", "shard"), None),
            P(("rep", "shard"), None),
            P(("rep", "shard"), None),
            P(None, ("rep", "shard")),
            P(("rep", "shard"), None),
            P(("rep", "shard"), None),
            P(("rep", "shard"), None),
            P(("rep", "shard"), None),
            P(None, ("rep", "shard")),
            P(("rep", "shard"), None),
            P(("rep", "shard"), None),
            P(("rep", "shard"), None),
            P(("rep", "shard"), None),
            P(None, ("rep", "shard")),
            P(("rep", "shard"), None),
            P(("rep", "shard"), None),
            P(("rep", "shard"), None),
            P(("rep", "shard"), None),
            P(None, ("rep", "shard")),
        ),
        check_vma=False,
    )
```

profile of v0, /device:TPU:0, one launch (start us, length us, event | category | flops | bytes accessed | tf_op | source)
XLA Modules:
  0.0 970.5 jit_solution(3823819101333165597)
XLA Ops:
  7.3 1.1 convert_element_type.84
  8.3 1.1 convert_element_type.85
  9.4 0.8 pad_maximum_fusion.4
  10.3 0.9 convert_element_type.93
  11.2 1.1 convert_element_type.94
  12.3 0.2 reshape.256
  12.4 0.7 pad_maximum_fusion.5
  13.3 74.3 %all-gather = f32[32,32,13]{1,2,0:T(8,128)S(1)} all-gather(f32[1,32,13]{1,2,0:T(8,128)S(1)} %bitcast.115), channel_id=1, replica_groups=mesh['rep'=8,'shard'=4] {'rep','shard'}, dimensions={0}, use_global_device_ids=true | all-gather | bytes 54912 | tf_op jit(solution)/shard_map/all_gather | solution.py:130
  87.6 0.1 reshape.269
  87.9 0.2 multiply_reduce_fusion.5
  88.3 33.2 %all-gather.6.cloned.1.call-done = bf16[1024,7168]{1,0:T(8,128)(2,1)} async-done(((bf16[32,7168]{1,0:T(8,128)(2,1)}), bf16[1024,7168]{1,0:T(8,128)(2,1)}) %all-gather.6.cloned.1.call-update) | async-done | bytes 14680080 | tf_op jit(solution)/shard_map/all_gather | solution.py:144
  121.5 3.8 fusion.14
  125.5 1.1 copy-done.13
  126.5 0.2 copy.58
  126.7 0.2 copy.59
  127.0 0.7 pad_maximum_fusion.7
  127.9 1.8 slice.208
  129.9 80.1 %all-gather.12.cloned.1.call-done = bf16[1024,5120]{1,0:T(8,128)(2,1)} async-done(((bf16[32,5120]{1,0:T(8,128)(2,1)}), bf16[1024,5120]{1,0:T(8,128)(2,1)}) %all-gather.12.cloned.1.call-update) | async-done | bytes 10485776 | tf_op jit(solution)/shard_map/all_gather | solution.py:187
  210.0 2.3 fusion.45
  212.4 28.5 %all-gather.10.cloned.1.call-done = bf16[512,1024]{0,1:T(8,128)(2,1)} async-done(((bf16[128,1024]{0,1:T(8,128)(2,1)}), bf16[512,1024]{0,1:T(8,128)(2,1)}) %all-gather.10.cloned.1.call-update) | async-done | bytes 1048592 | tf_op jit(solution)/shard_map/all_gather | solution.py:161
  240.9 2.1 fusion.17
  243.0 1.9 copy-done.1
  245.0 1.2 fusion.12
  246.2 23.0 %all-gather.8.cloned.1.call-done = bf16[512,1024]{1,0:T(8,128)(2,1)} async-done(((bf16[128,1024]{1,0:T(8,128)(2,1)}), bf16[512,1024]{1,0:T(8,128)(2,1)}) %all-gather.8.cloned.1.call-update) | async-done | bytes 1048592 | tf_op jit(solution)/shard_map/all_gather | solution.py:162
  269.2 1.5 copy.57
  270.7 4.5 multiply_reduce_fusion.4
  275.1 1.7 multiply_convert_fusion
  276.9 1.3 copy-done.4
  278.2 1.8 fusion.59
  280.1 4.7 fusion.22
  284.8 0.2 reduce-scatter.13.cloned.1.call-start
  285.1 8.0 slice.149
  293.0 14.0 %reshape.257 = bf16[4096,1024]{1,0:T(8,128)(2,1)} reshape(bf16[1024,4096]{1,0:T(8,128)(2,1)} %slice.149) | data formatting | bytes 16777216 | tf_op jit(solution)/shard_map/reshape | solution.py:190
  307.0 4.9 fusion.9
  312.0 0.9 copy-done
  312.9 4.2 fusion.82
  317.1 8.1 fusion.72
  325.2 20.3 %reshape.264 = f32[1024,4096]{1,0:T(8,128)} reshape(f32[4096,1024]{1,0:T(8,128)} %fusion.72) | data formatting | bytes 33554432 | tf_op jit(solution)/shard_map/reshape | solution.py:275
  345.5 9.7 fusion.53
  355.1 0.8 convolution_bitcast_fusion.1
  356.0 0.8 slice.154
  356.7 2.6 fusion.83
  359.4 1.0 slice.157
  360.4 0.9 multiply_add_fusion.6
  361.3 1.9 pad_maximum_fusion.2
  363.2 5.9 reduce-scatter.9.cloned.1.call-done
  369.0 1.7 fusion.49
  370.8 5.4 fusion.4
  376.2 7.5 multiply_reduce_fusion
  383.7 1.0 copy.62
  384.8 7.7 fusion.61
  392.5 34.0 %pad_maximum_fusion = f32[1024,12288]{1,0:T(8,128)} fusion(f32[1024,4096]{1,0:T(8,128)} %reshape.264, f32[1024,1024]{1,0:T(8,128)} %fusion.83, f32[1024,4096]{1,0:T(8,128)} %fusion.53, f32[1024,3072]{1,0:T(8,128)} %fusion.61), kind=kLoop, calls=%fused_computation | loop fusion | flops 37748736 | bytes 100663296 | tf_op jit(solution)/shard_map/concatenate | solution.py:275
  426.5 4.8 fusion.73
  431.4 3.0 fusion.42
  434.5 1.1 multiply_add_fusion.2
  435.6 83.1 %reduce-scatter.13.cloned.1.call-done = f32[32,13]{1,0:T(8,128)} async-done(((f32[1024,13]{1,0:T(8,128)}), f32[32,13]{1,0:T(8,128)}) %reduce-scatter.13.cloned.1.call-update) | async-done | bytes 1680
  518.7 0.8 copy.63
  519.5 0.6 multiply_subtract_fusion.6
  520.1 433.9 %reduce-scatter.11.cloned.1.call-done = f32[32,12288]{1,0:T(8,128)} async-done(((f32[1024,12288]{1,0:T(8,128)}), f32[32,12288]{1,0:T(8,128)}) %reduce-scatter.11.cloned.1.call-update) | async-done | bytes 1572880 | tf_op jit(solution)/shard_map/reduce_scatter | solution.py:274
  954.0 2.6 multiply_subtract_fusion.1
  956.7 0.1 reshape.265
  956.8 2.9 multiply_subtract_fusion
  959.7 1.7 multiply_subtract_fusion.3
  961.5 2.2 multiply_subtract_fusion.2
  (104 shorter events, 1.4 us)
Async XLA Ops:
  7.2 6.1 copy-start.27
  7.2 80.6 %copy-start.3 = (f32[128,1024]{1,0:T(8,128)S(1)}, f32[128,1024]{1,0:T(8,128)}, u32[]{:S(2)}) copy-start(f32[128,1024]{1,0:T(8,128)} %param.18) | copy-start | bytes 1572868
  7.2 114.3 %all-gather.6.cloned.1.call-start = ((), (), s32[]{:S(2)}) async-start(), calls=%async_computation.4 | async-start | bytes 15138816 | tf_op jit(solution)/shard_map/all_gather | solution.py:144
  10.2 199.8 %all-gather.12.cloned.1.call-start = ((), (), s32[]{:S(2)}) async-start(), calls=%async_computation.7 | async-start | bytes 10813440 | tf_op jit(solution)/shard_map/all_gather | solution.py:187
  13.2 227.7 %all-gather.10.cloned.1.call-start = ((), (), s32[]{:S(2)}) async-start(), calls=%async_computation.6 | async-start | bytes 1310720 | tf_op jit(solution)/shard_map/all_gather | solution.py:161
  125.4 1.2 copy-start.13
  125.4 2.5 copy-start.31
  125.4 4.5 copy-start.10
  127.8 141.4 %all-gather.8.cloned.1.call-start = ((), (), s32[]{:S(2)}) async-start(), calls=%async_computation.5 | async-start | bytes 1310720 | tf_op jit(solution)/shard_map/all_gather | solution.py:162
  129.7 229.7 %reduce-scatter.7.cloned.1.call-start = ((), (), s32[]{:S(2)}) async-start(), calls=%async_computation.8 | async-start | bytes 2621440 | tf_op jit(solution)/shard_map/reduce_scatter | solution.py:229
  243.0 2.0 copy-start.1
  270.7 4.5 copy-start.2
  276.9 1.3 copy-start.4
  280.1 89.0 %reduce-scatter.9.cloned.1.call-start = ((), (), s32[]{:S(2)}) async-start(), calls=%async_computation.9 | async-start | bytes 2621440 | tf_op jit(solution)/shard_map/reduce_scatter | solution.py:230
  284.8 233.8 %reduce-scatter.13.cloned.1.call-start = ((), (), s32[]{:S(2)}) async-start(), calls=%async_computation.11 | async-start | bytes 540672
  307.0 5.8 copy-start
  345.4 9.7 copy-start.5
  345.4 9.7 copy-start.6
  355.1 1.6 copy-start.15
  370.7 5.4 copy-start.14
  376.2 7.5 copy-start.19
  384.8 569.3 %reduce-scatter.11.cloned.1.call-start = ((), (), s32[]{:S(2)}) async-start(), calls=%async_computation.10 | async-start | bytes 51904512 | tf_op jit(solution)/shard_map/reduce_scatter | solution.py:274
  426.5 4.9 copy-start.16
  431.3 3.2 copy-start.11
  431.3 3.2 copy-start.20
  431.3 3.2 copy-start.21
  431.3 88.1 %copy-start.29 = (f32[13,32]{1,0:T(8,128)S(1)}, f32[13,32]{1,0:T(8,128)}, u32[]{:S(2)}) copy-start(f32[13,32]{1,0:T(8,128)} %param.30) | copy-start | bytes 4996
  431.3 88.1 %copy-start.30 = (f32[13,32]{1,0:T(8,128)S(1)}, f32[13,32]{1,0:T(8,128)}, u32[]{:S(2)}) copy-start(f32[13,32]{1,0:T(8,128)} %param.35) | copy-start | bytes 4996
  431.3 522.7 %copy-start.7 = (f32[32,4096]{1,0:T(8,128)S(1)}, f32[32,4096]{1,0:T(8,128)}, u32[]{:S(2)}) copy-start(f32[32,4096]{1,0:T(8,128)} %param.23) | copy-start | bytes 1572868
  431.4 522.7 %copy-start.17 = (f32[32,4096]{1,0:T(8,128)S(1)}, f32[32,4096]{1,0:T(8,128)}, u32[]{:S(2)}) copy-start(f32[32,4096]{1,0:T(8,128)} %param.28) | copy-start | bytes 1572868
  431.4 522.7 %copy-start.18 = (f32[32,4096]{1,0:T(8,128)S(1)}, f32[32,4096]{1,0:T(8,128)}, u32[]{:S(2)}) copy-start(f32[32,4096]{1,0:T(8,128)} %param.33) | copy-start | bytes 1572868
  434.5 522.3 %copy-start.8 = (f32[128,1024]{1,0:T(8,128)S(1)}, f32[128,1024]{1,0:T(8,128)}, u32[]{:S(2)}) copy-start(f32[128,1024]{1,0:T(8,128)} %param.24) | copy-start | bytes 1572868
  519.5 440.3 %copy-start.28 = (f32[13,32]{1,0:T(8,128)}, f32[13,32]{1,0:T(8,128)S(1)}, u32[]{:S(2)}) copy-start(f32[13,32]{1,0:T(8,128)S(1)} %copy.63) | copy-start | bytes 4996
  520.1 439.6 %copy-start.22 = (f32[32,1024]{1,0:T(8,128)S(1)}, f32[32,1024]{1,0:T(8,128)}, u32[]{:S(2)}) copy-start(f32[32,1024]{1,0:T(8,128)} %param.22) | copy-start | bytes 393220
  520.1 439.6 %copy-start.25 = (f32[32,1024]{1,0:T(8,128)S(1)}, f32[32,1024]{1,0:T(8,128)}, u32[]{:S(2)}) copy-start(f32[32,1024]{1,0:T(8,128)} %param.27) | copy-start | bytes 393220
  520.1 439.6 %copy-start.26 = (f32[32,1024]{1,0:T(8,128)S(1)}, f32[32,1024]{1,0:T(8,128)}, u32[]{:S(2)}) copy-start(f32[32,1024]{1,0:T(8,128)} %param.32) | copy-start | bytes 393220
  956.6 4.8 copy-start.12
  956.6 4.8 copy-start.23
  956.7 4.8 copy-start.24
  956.8 6.9 copy-start.9
Sparse Core Ops, SparseCore 0:
  11.5 110.0 all-gather.5
  124.9 85.0 all-gather.11
  212.2 28.6 all-gather.9
  242.9 26.2 all-gather.7
  280.2 43.3 reduce-scatter.6
  325.8 43.1 reduce-scatter.8
  384.9 133.7 reduce-scatter.12
  526.2 427.7 reduce-scatter.10
where the time goes:
time: 972 us; the launch traced here: 971 us
  waiting for transfers between devices  688 us (71%)
  matrix products  79.6 us (8%)
  blocking collectives  74.3 us (8%)
  other arithmetic  58 us (6%)
  local copies, waits for them, and re-layouts  55.7 us (6%)
  between operations  14.7 us (2%)
    reduce_scatter x1, waiting for transfers between devices, shards(): lax.psum_scatter(jnp.concatenate([term_qkv, term_up, term_out, term_down....  434 us
    unnamed x9, waiting for transfers between devices  83.2 us
    all_gather x1, waiting for transfers between devices, shards(): out_whole = lax.all_gather(out_table, ('rep', 'shard'), axis=0, tiled=True)  80.1 us
    all_gather x1, blocking collectives, shards(): vec_all = lax.all_gather(vectors, ('rep', 'shard'), axis=1, tiled=True)  74.3 us
    concatenate x1, other arithmetic, shards(): jnp.concatenate([term_qkv, term_up, term_out, term_down.reshape(D, per_ro...  34 us
    all_gather x1, waiting for transfers between devices, shards(): in_whole = lax.all_gather(in_table, ('rep', 'shard'), axis=0, tiled=True)  33.2 us
    all_gather x1, waiting for transfers between devices, shards(): lax.all_gather(key16, 'shard', axis=0, tiled=True)  28.5 us
    dot_general x4, matrix products, contract_rows(): lax.dot_general(left, right, (((0,), (0,)), ((), ())), preferred_element_...  28.1 us
  transfers between devices with their start and end apart: 8, of which 7 were waited for; matrix products, arithmetic and copies ran while one was open for 15% of the time, Pallas kernels for 0%

commit v1 on v0

--- a/solution.py
+++ b/solution.py
@@ -18,6 +18,27 @@
 ROPE_BASE = 10000.0
 INV_ROOT_TWO = 0.7071067811865476
 INV_ROOT_TAU = 0.3989422804014327
+
+
+def ring_gather(x, axis, dim):
+    size, index, rows = (lax.axis_size(axis), lax.axis_index(axis), x.shape[dim])
+    right = [(i, (i + 1) % size) for i in range(size)]
+    left = [(i, (i - 1) % size) for i in range(size)]
+    whole = jnp.zeros((*x.shape[:dim], size * rows, *x.shape[dim + 1 :]), x.dtype)
+    whole = lax.dynamic_update_slice_in_dim(whole, x, index * rows, axis=dim)
+    from_left = from_right = x
+    halfway = size // 2
+    for step in range(1, halfway + 1):
+        from_left = lax.ppermute(from_left, axis, right)
+        whole = lax.dynamic_update_slice_in_dim(
+            whole, from_left, (index - step) % size * rows, axis=dim
+        )
+        if step < size - halfway:
+            from_right = lax.ppermute(from_right, axis, left)
+            whole = lax.dynamic_update_slice_in_dim(
+                whole, from_right, (index + step) % size * rows, axis=dim
+            )
+    return whole
 
 
 def layer_norm(values, gain, shift):
@@ -159,7 +180,7 @@
     value16 = qkv_lin[:, 2 * D :].astype(bf16)
     keys_all, values_all = (
         lax.all_gather(key16, "shard", axis=0, tiled=True),
-        lax.all_gather(value16, "shard", axis=0, tiled=True),
+        ring_gather(value16, "shard", 0),
     )
     keys3 = keys_all.reshape(seq_len, HEADS, head_dim)
     values3 = values_all.reshape(seq_len, HEADS, head_dim)

time: 972 us -> 948 us (0.975)
  waiting for transfers between devices: 688 us -> 659 us
    all_gather x1 -> x0, waiting for transfers between devices: 23 us -> none  [shards(): lax.all_gather(value16, 'shard', axis=0, tiled=True)]
    all_gather x1, waiting for transfers between devices: 28.5 us -> 16.1 us  [shards(): lax.all_gather(key16, 'shard', axis=0, tiled=True)]
    unnamed x9 -> x8, waiting for transfers between devices: 83.2 us -> 82.7 us
  transfers between devices with their start and end apart: 8 -> 10, of which waited for: 7 -> 7; matrix products, arithmetic and copies ran while one was open for 15% -> 16% of each run, Pallas kernels for 0% -> 0%
where the time goes in v1:
time: 948 us; the launch traced here: 947 us
  waiting for transfers between devices  659 us (70%)
  matrix products  77.5 us (8%)
  blocking collectives  74.3 us (8%)
  other arithmetic  58.6 us (6%)
  local copies, waits for them, and re-layouts  56.5 us (6%)
  between operations  15 us (2%)
    reduce_scatter x1, waiting for transfers between devices, shards(): lax.psum_scatter(jnp.concatenate([term_qkv, term_up, term_out, term_down....  434 us
    unnamed x8, waiting for transfers between devices  82.7 us
    all_gather x1, waiting for transfers between devices, shards(): out_whole = lax.all_gather(out_table, ('rep', 'shard'), axis=0, tiled=True)  81.8 us
    all_gather x1, blocking collectives, shards(): vec_all = lax.all_gather(vectors, ('rep', 'shard'), axis=1, tiled=True)  74.3 us
    concatenate x1, other arithmetic, shards(): jnp.concatenate([term_qkv, term_up, term_out, term_down.reshape(D, per_ro...  34.1 us
    all_gather x1, waiting for transfers between devices, shards(): in_whole = lax.all_gather(in_table, ('rep', 'shard'), axis=0, tiled=True)  32.6 us
    dot_general x4, matrix products, contract_rows(): lax.dot_general(left, right, (((0,), (0,)), ((), ())), preferred_element_...  28.1 us
    reshape x1, local copies, waits for them, and re-layouts, shards(): term_down.reshape(D, per_row * D)  20.4 us
  transfers between devices with their start and end apart: 10, of which 7 were waited for; matrix products, arithmetic and copies ran while one was open for 16% of the time, Pallas kernels for 0%

profile of v1, /device:TPU:0, one launch (start us, length us, event | category | flops | bytes accessed | tf_op | source)
XLA Modules:
  0.0 946.9 jit_solution(17721631060173392767)
XLA Ops:
  7.3 1.1 convert_element_type.84
  8.3 1.1 convert_element_type.85
  9.4 0.8 pad_maximum_fusion.4
  10.3 0.9 convert_element_type.93
  11.2 1.1 convert_element_type.94
  12.4 0.7 pad_maximum_fusion.5
  13.3 74.3 %all-gather = f32[32,32,13]{1,2,0:T(8,128)S(1)} all-gather(f32[1,32,13]{1,2,0:T(8,128)S(1)} %bitcast.115), channel_id=1, replica_groups=mesh['rep'=8,'shard'=4] {'rep','shard'}, dimensions={0}, use_global_device_ids=true | all-gather | bytes 54912 | tf_op jit(solution)/shard_map/all_gather | solution.py:151
  88.3 0.6 fusion.82
  88.9 32.6 %all-gather.5.cloned.1.call-done = bf16[1024,7168]{1,0:T(8,128)(2,1)} async-done(((bf16[32,7168]{1,0:T(8,128)(2,1)}), bf16[1024,7168]{1,0:T(8,128)(2,1)}) %all-gather.5.cloned.1.call-update) | async-done | bytes 14680080 | tf_op jit(solution)/shard_map/all_gather | solution.py:165
  121.5 3.8 fusion.14
  125.5 1.1 copy-done.12
  127.1 0.7 pad_maximum_fusion.7
  128.1 0.6 fusion.81
  128.8 1.1 slice.208
  129.8 0.7 collective-permute-start
  130.5 3.2 collective-permute-start.1
  133.7 81.8 %all-gather.9.cloned.1.call-done = bf16[1024,5120]{1,0:T(8,128)(2,1)} async-done(((bf16[32,5120]{1,0:T(8,128)(2,1)}), bf16[1024,5120]{1,0:T(8,128)(2,1)}) %all-gather.9.cloned.1.call-update) | async-done | bytes 10485776 | tf_op jit(solution)/shard_map/all_gather | solution.py:208
  215.5 2.3 fusion.45
  218.0 1.4 collective-permute-start.2
  219.6 1.0 copy-done.14
  221.0 0.7 constant_dynamic-update-slice_fusion.2
  221.7 0.7 constant_dynamic-update-slice_fusion.1
  222.5 6.1 collective-permute-done.2
  228.7 0.8 constant_dynamic-update-slice_fusion
  229.5 16.1 %all-gather.7.cloned.1.call-done = bf16[512,1024]{0,1:T(8,128)(2,1)} async-done(((bf16[128,1024]{0,1:T(8,128)(2,1)}), bf16[512,1024]{0,1:T(8,128)(2,1)}) %all-gather.7.cloned.1.call-update) | async-done | bytes 1048592 | tf_op jit(solution)/shard_map/all_gather | solution.py:182
  245.6 2.2 fusion.17
  247.8 1.2 fusion.12
  249.0 2.3 multiply_reduce_fusion.4
  251.3 1.7 multiply_convert_fusion
  253.1 1.3 copy-done.3
  254.4 1.8 fusion.59
  256.2 4.7 fusion.22
  261.2 8.1 slice.149
  269.4 14.0 %reshape.257 = bf16[4096,1024]{1,0:T(8,128)(2,1)} reshape(bf16[1024,4096]{1,0:T(8,128)(2,1)} %slice.149) | data formatting | bytes 16777216 | tf_op jit(solution)/shard_map/reshape | solution.py:211
  283.3 4.9 fusion.9
  288.2 0.9 copy-done
  289.1 4.2 fusion.83
  293.3 8.1 fusion.73
  301.5 20.4 %reshape.264 = f32[1024,4096]{1,0:T(8,128)} reshape(f32[4096,1024]{1,0:T(8,128)} %fusion.73) | data formatting | bytes 33554432 | tf_op jit(solution)/shard_map/reshape | solution.py:296
  321.8 9.7 %fusion.53 = f32[1024,4096]{1,0:T(8,128)} fusion(bf16[128,4096]{1,0:T(8,128)(2,1)} %get-tuple-element.82, f32[1024]{0:T(1024)S(1)} %bitcast.110, f32[1024]{0:T(1024)S(1)} %bitcast.102, f32[128,1024]{1,0:T(8,128)S(1)} %copy-done.2, f32[128]{0:T(128)S(1)} %copy-done.41, f32[128]{0:T(128)S(1)} %copy-done.37), kind=kOutput, calls=%fused_computation.64 | convolution fusion | flops 1074397184 | bytes 18359296 | tf_op jit(solution)/shard_map/dot_general | solution.py:112
  331.5 0.8 convolution_bitcast_fusion.1
  332.3 0.8 slice.154
  333.1 2.7 fusion.84
  335.8 1.0 slice.157
  336.8 0.9 multiply_add_fusion.6
  337.7 1.9 pad_maximum_fusion.2
  339.6 5.9 reduce-scatter.9.cloned.1.call-done
  345.5 1.7 fusion.49
  347.3 5.4 fusion.4
  352.7 7.5 multiply_reduce_fusion
  360.2 1.0 copy.70
  361.3 7.6 fusion.61
  369.0 34.1 %pad_maximum_fusion = f32[1024,12288]{1,0:T(8,128)} fusion(f32[1024,4096]{1,0:T(8,128)} %reshape.264, f32[1024,1024]{1,0:T(8,128)} %fusion.84, f32[1024,4096]{1,0:T(8,128)} %fusion.53, f32[1024,3072]{1,0:T(8,128)} %fusion.61), kind=kLoop, calls=%fused_computation | loop fusion | flops 37748736 | bytes 100663296 | tf_op jit(solution)/shard_map/concatenate | solution.py:296
  403.1 4.8 fusion.74
  408.0 3.0 fusion.42
  411.1 1.1 multiply_add_fusion.2
  412.2 82.6 %reduce-scatter.13.cloned.1.call-done = f32[32,13]{1,0:T(8,128)} async-done(((f32[1024,13]{1,0:T(8,128)}), f32[32,13]{1,0:T(8,128)}) %reduce-scatter.13.cloned.1.call-update) | async-done | bytes 1680
  494.8 0.8 copy.71
  495.6 0.6 multiply_subtract_fusion.6
  496.2 434.1 %reduce-scatter.11.cloned.1.call-done = f32[32,12288]{1,0:T(8,128)} async-done(((f32[1024,12288]{1,0:T(8,128)}), f32[32,12288]{1,0:T(8,128)}) %reduce-scatter.11.cloned.1.call-update) | async-done | bytes 1572880 | tf_op jit(solution)/shard_map/reduce_scatter | solution.py:295
  930.4 2.6 multiply_subtract_fusion.1
  933.2 2.9 multiply_subtract_fusion
  936.1 1.7 multiply_subtract_fusion.3
  937.8 2.2 multiply_subtract_fusion.2
  (141 shorter events, 3.4 us)
Async XLA Ops:
  7.2 6.1 copy-start.33
  7.2 80.6 %copy-start.2 = (f32[128,1024]{1,0:T(8,128)S(1)}, f32[128,1024]{1,0:T(8,128)}, u32[]{:S(2)}) copy-start(f32[128,1024]{1,0:T(8,128)} %param.18) | copy-start | bytes 1572868
  7.2 114.3 %all-gather.5.cloned.1.call-start = ((), (), s32[]{:S(2)}) async-start(), calls=%async_computation.4 | async-start | bytes 15138816 | tf_op jit(solution)/shard_map/all_gather | solution.py:165
  10.2 205.3 %all-gather.9.cloned.1.call-start = ((), (), s32[]{:S(2)}) async-start(), calls=%async_computation.6 | async-start | bytes 10813440 | tf_op jit(solution)/shard_map/all_gather | solution.py:208
  13.2 232.3 %all-gather.7.cloned.1.call-start = ((), (), s32[]{:S(2)}) async-start(), calls=%async_computation.5 | async-start | bytes 1310720 | tf_op jit(solution)/shard_map/all_gather | solution.py:182
  87.9 37.4 %copy-start.36 = (f32[128]{0:T(128)}, f32[128]{0:T(128)S(1)}, u32[]{:S(2)}) copy-start(f32[128]{0:T(128)S(1)} %broadcast_multiply_fusion.4) | copy-start | bytes 1540
  88.2 37.2 %copy-start.40 = (f32[128]{0:T(128)}, f32[128]{0:T(128)S(1)}, u32[]{:S(2)}) copy-start(f32[128]{0:T(128)S(1)} %add_rsqrt_fusion) | copy-start | bytes 1540
  88.3 38.7 %copy-start.28 = (f32[128,8]{0,1:T(8,128)}, f32[128,8]{0,1:T(8,128)S(1)}, u32[]{:S(2)}) copy-start(f32[128,8]{0,1:T(8,128)S(1)} %get-tuple-element.74) | copy-start | bytes 12292
  88.3 38.7 %copy-start.30 = (f32[128,8]{0,1:T(8,128)}, f32[128,8]{0,1:T(8,128)S(1)}, u32[]{:S(2)}) copy-start(f32[128,8]{0,1:T(8,128)S(1)} %get-tuple-element.75) | copy-start | bytes 12292
  125.4 1.2 copy-start.12
  125.4 2.5 copy-start.44
  125.4 2.7 copy-start.9
  127.8 207.9 %reduce-scatter.7.cloned.1.call-start = ((), (), s32[]{:S(2)}) async-start(), calls=%async_computation.7 | async-start | bytes 2621440 | tf_op jit(solution)/shard_map/reduce_scatter | solution.py:250
  129.8 88.2 %collective-permute-start = (bf16[128,1024]{1,0:T(8,128)(2,1)S(1)}, bf16[128,1024]{1,0:T(8,128)(2,1)S(1)}, u32[]{:S(2)}, u32[]{:S(2)}) collective-permute-start(bf16[128,1024]{1,0:T(8,128)(2,1)S(1)} %slice.208), channel_id=1, source_target_pairs={{0,1},{1,2},{2,3},{3,0},{4,5},{5,6},{6,7},{7,4},{8,9},{9,10},{10,1... | collective-permute-start | bytes 786440 | tf_op jit(solution)/shard_map/ppermute | solution.py:32
  130.5 90.3 %collective-permute-start.1 = (bf16[128,1024]{1,0:T(8,128)(2,1)S(1)}, bf16[128,1024]{1,0:T(8,128)(2,1)S(1)}, u32[]{:S(2)}, u32[]{:S(2)}) collective-permute-start(bf16[128,1024]{1,0:T(8,128)(2,1)S(1)} %slice.208), channel_id=1, source_target_pairs={{0,3},{1,0},{2,1},{3,2},{4,7},{5,4},{6,5},{7,6},{8,11},{9,8},{10,9... | collective-permute-start | bytes 786440 | tf_op jit(solution)/shard_map/ppermute | solution.py:37
  218.0 10.5 %collective-permute-start.2 = (bf16[128,1024]{1,0:T(8,128)(2,1)S(1)}, bf16[128,1024]{1,0:T(8,128)(2,1)S(1)}, u32[]{:S(2)}, u32[]{:S(2)}) collective-permute-start(bf16[128,1024]{1,0:T(8,128)(2,1)S(1)} %collective-permute-done), channel_id=1, source_target_pairs={{0,1},{1,2},{2,3},{3,0},{4,5},{5,6},{6,7},{7,4},{8,9},{9,10},{10,1... | collective-permute-start | bytes 786440 | tf_op jit(solution)/shard_map/ppermute | solution.py:32
  219.5 1.0 copy-start.14
  245.6 3.5 copy-start.15
  247.8 3.5 copy-start.1
  253.0 1.3 copy-start.3
  256.2 89.4 %reduce-scatter.9.cloned.1.call-start = ((), (), s32[]{:S(2)}) async-start(), calls=%async_computation.8 | async-start | bytes 2621440 | tf_op jit(solution)/shard_map/reduce_scatter | solution.py:251
  261.0 233.8 %reduce-scatter.13.cloned.1.call-start = ((), (), s32[]{:S(2)}) async-start(), calls=%async_computation.10 | async-start | bytes 540672
  269.4 14.0 %copy-start.37 = (f32[128]{0:T(128)S(1)}, f32[128]{0:T(128)}, u32[]{:S(2)}) copy-start(f32[128]{0:T(128)} %copy-done.36) | copy-start | bytes 1540
  269.4 14.0 %copy-start.41 = (f32[128]{0:T(128)S(1)}, f32[128]{0:T(128)}, u32[]{:S(2)}) copy-start(f32[128]{0:T(128)} %copy-done.40) | copy-start | bytes 1540
  283.3 5.8 copy-start
  321.8 9.7 %copy-start.4 = (bf16[16,128,512]{2,1,0:T(8,128)(2,1)S(1)}, bf16[16,128,512]{2,1,0:T(8,128)(2,1)}, u32[]{:S(2)}) copy-start(bf16[16,128,512]{2,1,0:T(8,128)(2,1)} %copy-done.3) | copy-start | bytes 6291460
  321.8 9.7 %copy-start.5 = (bf16[512,1024]{0,1:T(8,128)(2,1)S(1)}, bf16[512,1024]{0,1:T(8,128)(2,1)}, u32[]{:S(2)}) copy-start(bf16[512,1024]{0,1:T(8,128)(2,1)} %all-gather.7.cloned.1.call-done) | copy-start | bytes 3145732
  331.5 1.6 copy-start.16
  331.5 5.3 copy-start.29
  331.5 5.3 copy-start.31
  347.2 5.4 copy-start.13
  352.7 7.5 copy-start.20
  352.7 7.5 copy-start.32
  361.3 569.1 %reduce-scatter.11.cloned.1.call-start = ((), (), s32[]{:S(2)}) async-start(), calls=%async_computation.9 | async-start | bytes 51904512 | tf_op jit(solution)/shard_map/reduce_scatter | solution.py:295
  403.0 4.9 copy-start.17
  403.1 4.9 copy-start.38
  403.1 4.9 copy-start.39
  407.9 3.2 copy-start.10
  407.9 3.2 copy-start.21
  407.9 3.2 copy-start.22
  407.9 87.7 %copy-start.34 = (f32[13,32]{1,0:T(8,128)S(1)}, f32[13,32]{1,0:T(8,128)}, u32[]{:S(2)}) copy-start(f32[13,32]{1,0:T(8,128)} %param.25) | copy-start | bytes 4996
  407.9 87.7 %copy-start.42 = (f32[13,32]{1,0:T(8,128)S(1)}, f32[13,32]{1,0:T(8,128)}, u32[]{:S(2)}) copy-start(f32[13,32]{1,0:T(8,128)} %param.30) | copy-start | bytes 4996
  407.9 87.7 %copy-start.43 = (f32[13,32]{1,0:T(8,128)S(1)}, f32[13,32]{1,0:T(8,128)}, u32[]{:S(2)}) copy-start(f32[13,32]{1,0:T(8,128)} %param.35) | copy-start | bytes 4996
  407.9 522.4 %copy-start.6 = (f32[32,4096]{1,0:T(8,128)S(1)}, f32[32,4096]{1,0:T(8,128)}, u32[]{:S(2)}) copy-start(f32[32,4096]{1,0:T(8,128)} %param.23) | copy-start | bytes 1572868
  407.9 522.4 %copy-start.18 = (f32[32,4096]{1,0:T(8,128)S(1)}, f32[32,4096]{1,0:T(8,128)}, u32[]{:S(2)}) copy-start(f32[32,4096]{1,0:T(8,128)} %param.28) | copy-start | bytes 1572868
  408.0 522.4 %copy-start.19 = (f32[32,4096]{1,0:T(8,128)S(1)}, f32[32,4096]{1,0:T(8,128)}, u32[]{:S(2)}) copy-start(f32[32,4096]{1,0:T(8,128)} %param.33) | copy-start | bytes 1572868
  411.1 522.1 %copy-start.7 = (f32[128,1024]{1,0:T(8,128)S(1)}, f32[128,1024]{1,0:T(8,128)}, u32[]{:S(2)}) copy-start(f32[128,1024]{1,0:T(8,128)} %param.24) | copy-start | bytes 1572868
  495.6 440.5 %copy-start.35 = (f32[13,32]{1,0:T(8,128)}, f32[13,32]{1,0:T(8,128)S(1)}, u32[]{:S(2)}) copy-start(f32[13,32]{1,0:T(8,128)S(1)} %copy.71) | copy-start | bytes 4996
  496.2 439.8 %copy-start.23 = (f32[32,1024]{1,0:T(8,128)S(1)}, f32[32,1024]{1,0:T(8,128)}, u32[]{:S(2)}) copy-start(f32[32,1024]{1,0:T(8,128)} %param.22) | copy-start | bytes 393220
  496.2 439.8 %copy-start.26 = (f32[32,1024]{1,0:T(8,128)S(1)}, f32[32,1024]{1,0:T(8,128)}, u32[]{:S(2)}) copy-start(f32[32,1024]{1,0:T(8,128)} %param.27) | copy-start | bytes 393220
  496.2 439.8 %copy-start.27 = (f32[32,1024]{1,0:T(8,128)S(1)}, f32[32,1024]{1,0:T(8,128)}, u32[]{:S(2)}) copy-start(f32[32,1024]{1,0:T(8,128)} %param.32) | copy-start | bytes 393220
  933.0 4.8 copy-start.11
  933.0 4.8 copy-start.24
  933.0 4.8 copy-start.25
  933.2 6.9 copy-start.8
Sparse Core Ops, SparseCore 0:
  11.5 110.0 all-gather.4
  124.9 90.5 all-gather.8
  217.7 27.8 all-gather.6
  256.3 43.7 reduce-scatter.6
  302.3 43.1 reduce-scatter.8
  361.4 133.3 reduce-scatter.12
  502.3 427.9 reduce-scatter.10
